TPU v7x, 32 devices: a whole 2x2x4 slice. The times are simulated.
32 devices in a mesh: tm: 2 (over x), lat: 4 (over y, core), lon: 4 (over z).
Axes of the slice: x: 2, y: 2, z: 4, core: 2. Of those that a mesh axis runs over, the one named last changes fastest.
Arguments:
- control: float32 [16, 8, 64, 512], P(None, None, 'lat', 'lon'), may hold values from -6 to 6
- ens_pert: bfloat16 [2, 16, 8, 64, 512], P('tm', None, None, 'lat', 'lon'), may hold values from -6 to 6
- lat_filter: bfloat16 [64, 64], replicated, may hold values from 0 to 2.5, as said below
- lon_filter: bfloat16 [512, 512], replicated, may hold values from 0 to 2.5, as said below
- interp_lat: float32 [128, 18], P('lat'), may hold values from -1.5 to 1.5
- interp_lon: float32 [1024, 130], P('lon'), may hold values from -0.5 to 0.5
- obs_cell: int32 [2, 2, 4, 4, 64], P('tm', None, 'lat', 'lon'), may hold values from 0 to 65535
- obs_count: int32 [2, 2, 4, 4], P('tm', None, 'lat', 'lon'), may hold values from 1 to 64, as said below
- obs_value: float32 [2, 2, 4, 4, 64], P('tm', None, 'lat', 'lon'), may hold values from -18 to 18
- obs_weight: float32 [2, 2, 4, 4, 64], P('tm', None, 'lat', 'lon'), may hold values from 0.1 to 0.4
Outputs:
- gradient: float32 [16, 8, 64, 512], P(None, None, 'lat', 'lon')
Inputs may be any that keep to these rules, and one draw needn't show every extreme that they name: `lat_filter`: within the latitude spreading matrix all entries are non-negative. `lon_filter`: entries are non-negative. `obs_count`: each count is at least 1 and at most 64; in every draw some count equals 64.
All inputs are finite; a program needn't handle non-finite values.
Results may differ from a plain program's by a relative error of at most 0.0003.
Values sent between devices are 32-bit elements; how exact they have to be, the bound alone decides.
No kernel may reach another device: no remote copies, remote signals or barrier semaphores. Data moves between devices by JAX's collectives and lax.ppermute only.
A program may use at most 64 MiB of HBM per device.

v0:
```python
import jax
import jax.numpy as jnp
from jax import lax
from jax.sharding import PartitionSpec as P

HIGHEST = lax.Precision.HIGHEST
DIRECTIONS = ((-1, -1), (-1, 0), (-1, 1), (0, -1), (0, 1), (1, -1), (1, 0), (1, 1))


def extended(array, sides, width):
    for axis, dim in sides:
        size, length = (lax.axis_size(axis), array.shape[dim])
        up = [(i, (i + 1) % size) for i in range(size)]
        down = [(j, i) for i, j in up]
        last = lax.slice_in_dim(array, length - width, length, axis=dim)
        first = lax.slice_in_dim(array, 0, width, axis=dim)
        before = lax.ppermute(last, axis, up)
        after = lax.ppermute(first, axis, down)
        array = jnp.concatenate([before, array, after], axis=dim)
    return array


def spread_field(source, lat_matrix, lon_matrix):
    members, levels, lat_rows, lon_cols = source.shape
    fields = members * levels
    stacked = source.reshape(fields, lat_rows, lon_cols)
    across = jnp.einsum(
        "ab,mbk->mak",
        lat_matrix,
        lax.all_to_all(stacked, "lat", split_axis=0, concat_axis=1, tiled=True),
        precision=HIGHEST,
    )
    halfway = lax.all_to_all(across, "lat", split_axis=1, concat_axis=0, tiled=True)
    column = lax.axis_index("lon") * lon_cols
    portion = lax.all_gather(halfway, "lon", axis=2, tiled=True)
    section = lax.dynamic_slice(lon_matrix, (column, 0), (lon_cols, portion.shape[2]))
    result = jnp.einsum("mak,ck->mac", portion, section, precision=HIGHEST)
    return result.reshape(members, levels, lat_rows, lon_cols)


def rim_region(offset, length):
    if offset < 0:
        return slice(0, 1)
    if offset > 0:
        return slice(length + 1, length + 2)
    return slice(1, length + 1)


def own_cells(offset, length):
    if offset < 0:
        return slice(0, 1)
    if offset > 0:
        return slice(length - 1, length)
    return slice(0, length)


def per_device(
    control,
    ens_pert,
    lat_filter,
    lon_filter,
    interp_lat,
    interp_lon,
    obs_cell,
    obs_count,
    obs_value,
    obs_weight,
):
    lat_matrix = lat_filter.astype(jnp.float32)
    lon_matrix = lon_filter.astype(jnp.float32)
    members = control.shape[0]
    slot_pert = ens_pert[0]
    share = members // lax.axis_size("tm")
    first = lax.axis_index("tm") * share
    mine = lax.dynamic_slice_in_dim(control, first, share, 0)
    spread_mine = spread_field(mine, lat_matrix, lon_matrix)
    weights_here = slot_pert.astype(jnp.float32)
    increment = jnp.sum(
        lax.all_gather(spread_mine, "tm", axis=0, tiled=True) * weights_here, axis=0
    )
    levels, lat_rows, lon_cols = increment.shape
    padded = extended(increment, (("lat", 1), ("lon", 2)), 1)
    lat_band = lax.axis_index("lat")
    edge_rows = jnp.arange(lat_rows + 2)
    dropped = (edge_rows == 0) & (lat_band == 0) | (edge_rows == lat_rows + 1) & (
        lat_band == lax.axis_size("lat") - 1
    )
    keeping = jnp.logical_not(dropped).astype(jnp.float32)[None, :, None]
    padded = padded * keeping
    rowwise = jnp.einsum("ip,lpq->liq", interp_lat, padded, precision=HIGHEST)
    finer = jnp.einsum("liq,jq->lij", rowwise, interp_lon, precision=HIGHEST)
    fine_rows = finer.shape[1]
    fine_cols = finer.shape[2]
    flat_field = finer.reshape(-1)
    slots_range = jnp.arange(obs_cell.shape[-1])
    usable = (slots_range < obs_count[..., None]).astype(jnp.float32)
    package = jnp.stack([obs_cell.astype(jnp.float32), obs_value, obs_weight * usable], axis=0)
    arrived = lax.all_to_all(package, "tm", split_axis=2, concat_axis=1, tiled=True)
    places = arrived[0].reshape(-1).astype(jnp.int32)
    targets = arrived[1].reshape(-1)
    weights = arrived[2].reshape(-1)
    seen = flat_field[places]
    departure = weights * (seen - targets)
    fine_grad = jnp.zeros_like(flat_field).at[places].add(departure)
    fine_grad = fine_grad.reshape(levels, fine_rows, fine_cols)
    pulled = jnp.einsum("jq,lij->liq", interp_lon, fine_grad, precision=HIGHEST)
    coarse_pad = jnp.einsum("ip,liq->lpq", interp_lat, pulled, precision=HIGHEST) * keeping
    outgoing = []
    for lat_step, lon_step in DIRECTIONS:
        holder = jnp.zeros((levels, lat_rows, lon_cols), jnp.float32)
        holder = holder.at[:, own_cells(lat_step, lat_rows), own_cells(lon_step, lon_cols)].set(
            coarse_pad[:, rim_region(lat_step, lat_rows), rim_region(lon_step, lon_cols)]
        )
        outgoing.append(holder)
    bundle = jnp.stack(outgoing, axis=0)
    incoming = extended(bundle, (("lat", 2), ("lon", 3)), 1)
    coarse_grad = coarse_pad[:, 1:-1, 1:-1]
    for number, (lat_step, lon_step) in enumerate(DIRECTIONS):
        coarse_grad = coarse_grad.at[
            :, own_cells(-lat_step, lat_rows), own_cells(-lon_step, lon_cols)
        ].add(incoming[number][:, rim_region(-lat_step, lat_rows), rim_region(-lon_step, lon_cols)])
    weights_here = slot_pert.astype(jnp.float32)
    share_grad = lax.psum_scatter(
        weights_here * coarse_grad[None], "tm", scatter_dimension=0, tiled=True
    )
    adjoint_mine = spread_field(share_grad, lat_matrix.T, lon_matrix.T)
    return control + lax.all_gather(adjoint_mine, "tm", axis=0, tiled=True)


def solution(mesh):
    placed = (
        P(None, None, "lat", "lon"),
        P("tm", None, None, "lat", "lon"),
        P(),
        P(),
        P("lat", None),
        P("lon", None),
        P("tm", None, "lat", "lon", None),
        P("tm", None, "lat", "lon"),
        P("tm", None, "lat", "lon", None),
        P("tm", None, "lat", "lon", None),
    )
    return jax.shard_map(
        per_device,
        mesh=mesh,
        in_specs=placed,
        out_specs=P(None, None, "lat", "lon"),
        check_vma=False,
    )
```

profile of v0, /device:TPU:0, one launch (start us, length us, event | category | flops | bytes accessed | tf_op | source)
XLA Modules:
  0.0 265.9 jit_solution(17152153929202696150)
XLA Ops:
  7.7 12.9 %all_to_all.81 = f32[64,16,128]{2,1,0:T(8,128)S(1)} all-to-all(f32[64,16,128]{2,1,0:T(8,128)S(1)} %bitcast.107), channel_id=1, replica_groups=mesh['tm'=2,'lat'=4,'lon'=4] {'lat'}, dimensions={0} | all-to-all | bytes 1048576 | tf_op jit(solution)/shard_map/all_to_all | solution.py:30
  21.4 11.2 %all_to_all.82 = f32[16,64,128]{2,0,1:T(8,128)S(1)} all-to-all(f32[16,64,128]{2,0,1:T(8,128)S(1)} %copy.43), channel_id=1, replica_groups=mesh['tm'=2,'lat'=4,'lon'=4] {'lat'}, dimensions={1} | all-to-all | bytes 1048576 | tf_op jit(solution)/shard_map/all_to_all | solution.py:33
  33.7 46.6 %all-gather.5.cloned.1.call-done = f32[64,16,512]{2,1,0:T(8,128)} async-done(((f32[64,16,128]{2,1,0:T(8,128)}), f32[64,16,512]{2,1,0:T(8,128)}) %all-gather.5.cloned.1.call-update) | async-done | bytes 2097168 | tf_op jit(solution)/shard_map/all_gather | solution.py:35
  80.3 3.4 %fusion.16 = f32[64,16,128]{2,1,0:T(8,128)} fusion(f32[64,16,512]{2,1,0:T(8,128)} %all-gather.5.cloned.1.call-done, bf16[512,512]{1,0:T(8,128)(2,1)S(1)} %copy-done, s32[]{:T(128)S(6)} %select_n.20), kind=kOutput, calls=%fused_computation.35 | convolution fusion | flops 805306368 | bytes 2752516 | tf_op jit(solution)/shard_map/mak,ck->mac/dot_general | solution.py:37
  85.7 3.2 %all-to-all-start = ((f32[2,1,192]{2,1,0:T(1,128)}), f32[2,1,192]{2,1,0:T(1,128)S(1)}, u32[]{:S(2)}, u32[]{:S(2)}) async-start(f32[2,1,192]{2,1,0:T(1,128)} %reshape.675), calls=%async_computation | async-start | bytes 4096 | tf_op jit(solution)/shard_map/all_to_all | solution.py:98
  90.4 2.2 all-to-all-done
  93.5 9.9 %all-gather.7.cloned.1.call-done = f32[16,8,16,128]{3,2,1,0:T(8,128)} async-done(((f32[8,8,16,128]{3,2,1,0:T(8,128)}), f32[16,8,16,128]{3,2,1,0:T(8,128)}) %all-gather.7.cloned.1.call-update) | async-done | bytes 1048592 | tf_op jit(solution)/shard_map/all_gather | solution.py:79
  104.9 1.7 collective-permute-start.1
  108.0 1.5 collective-permute-start.2
  109.5 2.4 collective-permute-start.3
  112.1 3.1 %collective-permute-done.2 = f32[8,18,1]{2,1,0:T(8,128)S(1)} collective-permute-done((f32[8,18,1]{2,1,0:T(8,128)S(1)}, f32[8,18,1]{2,1,0:T(8,128)S(1)}, u32[]{:S(2)}, u32[]{:S(2)}) %collective-permute-start.2) | collective-permute-done | bytes 608 | tf_op jit(solution)/shard_map/ppermute | solution.py:17
  115.1 1.8 collective-permute-done.3
  124.5 1.6 collective-permute-start.5
  126.1 1.6 collective-permute-done.4
  130.2 2.6 collective-permute-start.7
  138.0 2.1 add_select_fusion
  140.1 1.4 scatter-add.44
  142.8 20.4 %reduce-scatter.2.cloned.1.call-done = f32[8,8,16,128]{3,2,1,0:T(8,128)} async-done(((f32[16,8,16,128]{3,2,1,0:T(8,128)}), f32[8,8,16,128]{3,2,1,0:T(8,128)}) %reduce-scatter.2.cloned.1.call-update) | async-done | bytes 524304 | tf_op jit(solution)/shard_map/reduce_scatter | solution.py:123
  163.2 12.3 %all_to_all.83 = f32[64,16,128]{2,1,0:T(8,128)S(1)} all-to-all(f32[64,16,128]{2,1,0:T(8,128)} %bitcast.117), channel_id=1, replica_groups=mesh['tm'=2,'lat'=4,'lon'=4] {'lat'}, dimensions={0} | all-to-all | bytes 1048576 | tf_op jit(solution)/shard_map/all_to_all | solution.py:30
  176.2 11.2 %all_to_all.84 = f32[16,64,128]{2,0,1:T(8,128)S(1)} all-to-all(f32[16,64,128]{2,0,1:T(8,128)S(1)} %copy.62), channel_id=1, replica_groups=mesh['tm'=2,'lat'=4,'lon'=4] {'lat'}, dimensions={1} | all-to-all | bytes 1048576 | tf_op jit(solution)/shard_map/all_to_all | solution.py:33
  188.5 45.4 %all-gather.9.cloned.1.call-done = f32[64,16,512]{2,1,0:T(8,128)} async-done(((f32[64,16,128]{2,1,0:T(8,128)}), f32[64,16,512]{2,1,0:T(8,128)}) %all-gather.9.cloned.1.call-update) | async-done | bytes 2097168 | tf_op jit(solution)/shard_map/all_gather | solution.py:35
  233.9 3.4 %fusion.14 = f32[64,16,128]{2,1,0:T(8,128)} fusion(f32[64,16,512]{2,1,0:T(8,128)} %all-gather.9.cloned.1.call-done, bf16[512,512]{1,0:T(8,128)(2,1)S(1)} %copy-done, s32[]{:T(128)S(6)} %select_n.20), kind=kOutput, calls=%fused_computation.33 | convolution fusion | flops 805306368 | bytes 2752516 | tf_op jit(solution)/shard_map/mak,ck->mac/dot_general | solution.py:37
  237.4 19.6 %all-gather.11.cloned.1.call-done = f32[16,8,16,128]{3,2,1,0:T(8,128)} async-done(((f32[8,8,16,128]{3,2,1,0:T(8,128)}), f32[16,8,16,128]{3,2,1,0:T(8,128)}) %all-gather.11.cloned.1.call-update) | async-done | bytes 1048592 | tf_op jit(solution)/shard_map/all_gather | solution.py:127
  257.0 2.3 add.122
  (125 shorter events, 28.3 us)
Async XLA Ops:
  6.5 73.7 %copy-start = (bf16[512,512]{1,0:T(8,128)(2,1)S(1)}, bf16[512,512]{1,0:T(8,128)(2,1)}, u32[]{:S(2)}) copy-start(bf16[512,512]{1,0:T(8,128)(2,1)} %param.45) | copy-start | bytes 1572868
  6.5 73.7 %all-gather.5.cloned.1.call-start = ((), (), s32[]{:S(2)}) async-start(), calls=%async_computation.6 | async-start | bytes 2621440 | tf_op jit(solution)/shard_map/all_gather | solution.py:35
  7.7 12.9 %copy-start.4 = (bf16[64,64]{1,0:T(8,128)(2,1)S(1)}, bf16[64,64]{1,0:T(8,128)(2,1)}, u32[]{:S(2)}) copy-start(bf16[64,64]{1,0:T(8,128)(2,1)} %param.44) | copy-start | bytes 24580
  33.6 69.9 %all-gather.7.cloned.1.call-start = ((), (), s32[]{:S(2)}) async-start(), calls=%async_computation.7 | async-start | bytes 1572864 | tf_op jit(solution)/shard_map/all_gather | solution.py:79
  33.6 50.1 %copy-start.7 = (f32[1,2,1,1,64]{4,3,2,1,0:T(1,128)S(1)}, f32[1,2,1,1,64]{4,3,2,1,0:T(1,128)}, u32[]{:S(2)}) copy-start(f32[1,2,1,1,64]{4,3,2,1,0:T(1,128)} %param.51) | copy-start | bytes 1540
  33.6 50.1 %copy-start.9 = (s32[1,2,1,1]{1,3,2,0:T(1,128)S(1)}, s32[1,2,1,1]{1,3,2,0:T(1,128)}, u32[]{:S(2)}) copy-start(s32[1,2,1,1]{1,3,2,0:T(1,128)} %param.49) | copy-start | bytes 28
  33.7 50.2 %copy-start.8 = (f32[1,2,1,1,64]{4,3,2,1,0:T(1,128)S(1)}, f32[1,2,1,1,64]{4,3,2,1,0:T(1,128)}, u32[]{:S(2)}) copy-start(f32[1,2,1,1,64]{4,3,2,1,0:T(1,128)} %param.50) | copy-start | bytes 1540
  33.7 56.0 %copy-start.10 = (s32[3]{0:T(128)S(1)}, s32[3]{0:T(128)}, u32[]{:S(2)}) copy-start(s32[3]{0:T(128)} %constant.430.clone.1) | copy-start | bytes 40
  33.7 69.7 %copy-start.2 = (bf16[1,16,8,16,128]{4,3,2,1,0:T(8,128)(2,1)S(1)}, bf16[1,16,8,16,128]{4,3,2,1,0:T(8,128)(2,1)}, u32[]{:S(2)}) copy-start(bf16[1,16,8,16,128]{4,3,2,1,0:T(8,128)(2,1)} %param.43) | copy-start | bytes 1572868
  83.7 33.2 %copy-start.5 = (f32[32,18]{0,1:T(8,128)S(1)}, f32[32,18]{0,1:T(8,128)}, u32[]{:S(2)}) copy-start(f32[32,18]{0,1:T(8,128)} %param.46) | copy-start | bytes 6916
  85.7 7.0 %all-to-all-start = ((f32[2,1,192]{2,1,0:T(1,128)}), f32[2,1,192]{2,1,0:T(1,128)S(1)}, u32[]{:S(2)}, u32[]{:S(2)}) async-start(f32[2,1,192]{2,1,0:T(1,128)} %reshape.675), calls=%async_computation | async-start | bytes 4096 | tf_op jit(solution)/shard_map/all_to_all | solution.py:98
  88.9 74.3 %reduce-scatter.2.cloned.1.call-start = ((), (), s32[]{:S(2)}) async-start(), calls=%async_computation.8 | async-start | bytes 1572864 | tf_op jit(solution)/shard_map/reduce_scatter | solution.py:123
  93.5 24.0 %copy-start.3 = (f32[256,130]{0,1:T(8,128)S(1)}, f32[256,130]{0,1:T(8,128)}, u32[]{:S(2)}) copy-start(f32[256,130]{0,1:T(8,128)} %param.47) | copy-start | bytes 399364
  104.8 3.1 %collective-permute-start = (f32[8,1,128]{2,1,0:T(1,128)S(1)}, f32[8,1,128]{2,1,0:T(1,128)S(1)}, u32[]{:S(2)}, u32[]{:S(2)}) collective-permute-start(f32[8,1,128]{2,1,0:T(1,128)S(1)} %get-tuple-element.222), channel_id=1, source_target_pairs={{0,4},{4,8},{8,12},{12,0},{1,5},{5,9},{9,13},{13,1},{2,6},{6,10},{... | collective-permute-start | bytes 12296 | tf_op jit(solution)/shard_map/ppermute | solution.py:17
  104.9 3.1 %collective-permute-start.1 = (f32[8,1,128]{2,1,0:T(1,128)S(1)}, f32[8,1,128]{2,1,0:T(1,128)S(1)}, u32[]{:S(2)}, u32[]{:S(2)}) collective-permute-start(f32[8,1,128]{2,1,0:T(1,128)S(1)} %get-tuple-element.223), channel_id=1, source_target_pairs={{4,0},{8,4},{12,8},{0,12},{5,1},{9,5},{13,9},{1,13},{6,2},{10,6},{... | collective-permute-start | bytes 12296 | tf_op jit(solution)/shard_map/ppermute | solution.py:18
  108.0 7.1 %collective-permute-start.2 = (f32[8,18,1]{2,1,0:T(8,128)S(1)}, f32[8,18,1]{2,1,0:T(8,128)S(1)}, u32[]{:S(2)}, u32[]{:S(2)}) collective-permute-start(f32[8,18,1]{2,1,0:T(8,128)S(1)} %get-tuple-element.220), channel_id=1, source_target_pairs={{0,1},{1,2},{2,3},{3,0},{4,5},{5,6},{6,7},{7,4},{8,9},{9,10},{10,1... | collective-permute-start | bytes 1736 | tf_op jit(solution)/shard_map/ppermute | solution.py:17
  109.5 7.5 %collective-permute-start.3 = (f32[8,18,1]{2,1,0:T(8,128)S(1)}, f32[8,18,1]{2,1,0:T(8,128)S(1)}, u32[]{:S(2)}, u32[]{:S(2)}) collective-permute-start(f32[8,18,1]{2,1,0:T(8,128)S(1)} %get-tuple-element.221), channel_id=1, source_target_pairs={{1,0},{2,1},{3,2},{0,3},{5,4},{6,5},{7,6},{4,7},{9,8},{10,9},{11,1... | collective-permute-start | bytes 1736 | tf_op jit(solution)/shard_map/ppermute | solution.py:18
  124.3 3.3 %collective-permute-start.4 = (f32[8,8,1,128]{3,1,2,0:T(8,128)S(1)}, f32[8,8,1,128]{3,1,2,0:T(8,128)S(1)}, u32[]{:S(2)}, u32[]{:S(2)}) collective-permute-start(f32[8,8,1,128]{3,1,2,0:T(8,128)S(1)} %get-tuple-element.211), channel_id=1, source_target_pairs={{0,4},{4,8},{8,12},{12,0},{1,5},{5,9},{9,13},{13,1},{2,6},{6,10},{... | collective-permute-start | bytes 98312 | tf_op jit(solution)/shard_map/ppermute | solution.py:17
  124.5 3.2 %collective-permute-start.5 = (f32[8,8,1,128]{3,1,2,0:T(8,128)S(1)}, f32[8,8,1,128]{3,1,2,0:T(8,128)S(1)}, u32[]{:S(2)}, u32[]{:S(2)}) collective-permute-start(f32[8,8,1,128]{3,1,2,0:T(8,128)S(1)} %get-tuple-element.212), channel_id=1, source_target_pairs={{4,0},{8,4},{12,8},{0,12},{5,1},{9,5},{13,9},{1,13},{6,2},{10,6},{... | collective-permute-start | bytes 98312 | tf_op jit(solution)/shard_map/ppermute | solution.py:18
  128.4 5.9 %collective-permute-start.6 = (f32[8,8,18,1]{2,1,3,0:T(8,128)S(1)}, f32[8,8,18,1]{2,1,3,0:T(8,128)S(1)}, u32[]{:S(2)}, u32[]{:S(2)}) collective-permute-start(f32[8,8,18,1]{2,1,3,0:T(8,128)S(1)} %copy.55), channel_id=1, source_target_pairs={{0,1},{1,2},{2,3},{3,0},{4,5},{5,6},{6,7},{7,4},{8,9},{9,10},{10,1... | collective-permute-start | bytes 13832 | tf_op jit(solution)/shard_map/ppermute | solution.py:17
  130.2 5.0 %collective-permute-start.7 = (f32[8,8,18,1]{2,1,3,0:T(8,128)S(1)}, f32[8,8,18,1]{2,1,3,0:T(8,128)S(1)}, u32[]{:S(2)}, u32[]{:S(2)}) collective-permute-start(f32[8,8,18,1]{2,1,3,0:T(8,128)S(1)} %copy.56), channel_id=1, source_target_pairs={{1,0},{2,1},{3,2},{0,3},{5,4},{6,5},{7,6},{4,7},{9,8},{10,9},{11,1... | collective-permute-start | bytes 13832 | tf_op jit(solution)/shard_map/ppermute | solution.py:18
  142.8 91.2 %all-gather.9.cloned.1.call-start = ((), (), s32[]{:S(2)}) async-start(), calls=%async_computation.9 | async-start | bytes 2621440 | tf_op jit(solution)/shard_map/all_gather | solution.py:35
  188.4 68.6 %copy-start.1 = (f32[16,8,16,128]{3,2,1,0:T(8,128)S(1)}, f32[16,8,16,128]{3,2,1,0:T(8,128)}, u32[]{:S(2)}) copy-start(f32[16,8,16,128]{3,2,1,0:T(8,128)} %param.42) | copy-start | bytes 3145732
  188.4 68.6 %all-gather.11.cloned.1.call-start = ((), (), s32[]{:S(2)}) async-start(), calls=%async_computation.10 | async-start | bytes 1572864 | tf_op jit(solution)/shard_map/all_gather | solution.py:127
  (1 other events, 12.3 us)
Sparse Core Ops, SparseCore 0:
  33.7 46.5 all-gather.4
  83.9 19.5 all-gather.6
  142.9 20.2 reduce-scatter.1
  188.6 45.3 all-gather.8
  237.5 19.4 all-gather.10
where the time goes:
time: 267 us; the launch traced here: 266 us
  waiting for transfers between devices  154 us (58%)
  blocking collectives  47.6 us (18%)
  local copies, waits for them, and re-layouts  15.1 us (6%)
  starting transfers between devices  14.7 us (6%)
  between operations  13.6 us (5%)
  other arithmetic  11.9 us (4%)
  matrix products  9.28 us (3%)
    all_gather x2, waiting for transfers between devices, spread_field(): portion = lax.all_gather(halfway, 'lon', axis=2, tiled=True)  92 us
    all_to_all x2, blocking collectives, spread_field(): lax.all_to_all(stacked, 'lat', split_axis=0, concat_axis=1, tiled=True)  25.1 us
    all_to_all x2, blocking collectives, spread_field(): lax.all_to_all(across, 'lat', split_axis=1, concat_axis=0, tiled=True)  22.4 us
    reduce_scatter x1, waiting for transfers between devices, per_device(): lax.psum_scatter(weights_here * coarse_grad[None], 'tm', scatter_dimensio...  20.4 us
    all_gather x1, waiting for transfers between devices, per_device(): return control + lax.all_gather(adjoint_mine, 'tm', axis=0, tiled=True)  19.6 us
    all_gather x1, waiting for transfers between devices, per_device(): lax.all_gather(spread_mine, 'tm', axis=0, tiled=True) * weights_here  9.88 us
    ppermute x4, starting transfers between devices, extended(): after = lax.ppermute(first, axis, down)  8.39 us
    ppermute x4, waiting for transfers between devices, extended(): before = lax.ppermute(last, axis, up)  7.34 us
  transfers between devices with their start and end apart: 14, of which 12 were waited for; matrix products, arithmetic and copies ran while one was open for 2% of the time, Pallas kernels for 0%

commit v1 on v0

--- a/solution.py
+++ b/solution.py
@@ -32,7 +32,12 @@
     )
     halfway = lax.all_to_all(across, "lat", split_axis=1, concat_axis=0, tiled=True)
     column = lax.axis_index("lon") * lon_cols
-    portion = lax.all_gather(halfway, "lon", axis=2, tiled=True)
+    ring = [halfway]
+    for hop in range(3):
+        ring.append(lax.ppermute(ring[-1], "lon", [(dev, (dev + 1) % 4) for dev in range(4)]))
+    portion = jnp.roll(
+        jnp.concatenate(ring[::-1], axis=2), (lax.axis_index("lon") + 1) * ring[0].shape[2], axis=2
+    )
     section = lax.dynamic_slice(lon_matrix, (column, 0), (lon_cols, portion.shape[2]))
     result = jnp.einsum("mak,ck->mac", portion, section, precision=HIGHEST)
     return result.reshape(members, levels, lat_rows, lon_cols)

time: 267 us -> 257 us (0.963)
  waiting for transfers between devices: 154 us -> 144 us
  starting transfers between devices: 14.7 us -> 17.8 us
    all_gather x2 -> x0, waiting for transfers between devices: 92 us -> none  [spread_field(): portion = lax.all_gather(halfway, 'lon', axis=2, tiled=True)]
    ppermute x0 -> x6, waiting for transfers between devices: none -> 82.5 us  [spread_field(): lax.ppermute(ring[-1], 'lon', [(dev, (dev + 1) % 4) for dev in range(4)])]
    ppermute x0 -> x6, starting transfers between devices: none -> 3.19 us  [spread_field(): lax.ppermute(ring[-1], 'lon', [(dev, (dev + 1) % 4) for dev in range(4)])]
  transfers between devices with their start and end apart: 14 -> 18, of which waited for: 12 -> 16; matrix products, arithmetic and copies ran while one was open for 2% -> 2% of each run, Pallas kernels for 0% -> 0%
where the time goes in v1:
time: 257 us
  waiting for transfers between devices  144 us (56%)
  blocking collectives  47.6 us (19%)
  starting transfers between devices  17.8 us (7%)
  local copies, waits for them, and re-layouts  13.6 us (5%)
  between operations  13.6 us (5%)
  other arithmetic  11.9 us (5%)
  matrix products  8.44 us (3%)
    ppermute x6, waiting for transfers between devices, spread_field(): lax.ppermute(ring[-1], 'lon', [(dev, (dev + 1) % 4) for dev in range(4)])  82.5 us
    all_to_all x2, blocking collectives, spread_field(): lax.all_to_all(stacked, 'lat', split_axis=0, concat_axis=1, tiled=True)  25.1 us
    all_to_all x2, blocking collectives, spread_field(): lax.all_to_all(across, 'lat', split_axis=1, concat_axis=0, tiled=True)  22.4 us
    reduce_scatter x1, waiting for transfers between devices, per_device(): lax.psum_scatter(weights_here * coarse_grad[None], 'tm', scatter_dimensio...  20.4 us
    all_gather x1, waiting for transfers between devices, per_device(): return control + lax.all_gather(adjoint_mine, 'tm', axis=0, tiled=True)  18.9 us
    all_gather x1, waiting for transfers between devices, per_device(): lax.all_gather(spread_mine, 'tm', axis=0, tiled=True) * weights_here  10 us
    ppermute x4, starting transfers between devices, extended(): after = lax.ppermute(first, axis, down)  8.39 us
    ppermute x4, waiting for transfers between devices, extended(): before = lax.ppermute(last, axis, up)  7.21 us
  transfers between devices with their start and end apart: 18, of which 16 were waited for; matrix products, arithmetic and copies ran while one was open for 2% of the time, Pallas kernels for 0%

profile of v1, /device:TPU:0, one launch (start us, length us, event | category | flops | bytes accessed | tf_op | source)
XLA Modules:
  0.0 256.5 jit_solution(712661554091124170)
XLA Ops:
  7.7 12.9 %all_to_all.81 = f32[64,16,128]{2,1,0:T(8,128)S(1)} all-to-all(f32[64,16,128]{2,1,0:T(8,128)S(1)} %bitcast.103), channel_id=1, replica_groups=mesh['tm'=2,'lat'=4,'lon'=4] {'lat'}, dimensions={0} | all-to-all | bytes 1048576 | tf_op jit(solution)/shard_map/all_to_all | solution.py:30
  21.4 11.2 %all_to_all.82 = f32[16,64,128]{2,0,1:T(8,128)S(1)} all-to-all(f32[16,64,128]{2,0,1:T(8,128)S(1)} %copy.43), channel_id=1, replica_groups=mesh['tm'=2,'lat'=4,'lon'=4] {'lat'}, dimensions={1} | all-to-all | bytes 1048576 | tf_op jit(solution)/shard_map/all_to_all | solution.py:33
  34.4 13.6 %collective-permute-done = f32[64,16,128]{2,1,0:T(8,128)S(1)} collective-permute-done((f32[64,16,128]{2,1,0:T(8,128)S(1)}, f32[64,16,128]{2,1,0:T(8,128)S(1)}, u32[]{:S(2)}, u32[]{:S(2)}) %collective-permute-start) | collective-permute-done | bytes 524320 | tf_op jit(solution)/shard_map/ppermute | solution.py:37
  48.0 14.3 %collective-permute-done.1 = f32[64,16,128]{2,1,0:T(8,128)S(1)} collective-permute-done((f32[64,16,128]{2,1,0:T(8,128)S(1)}, f32[64,16,128]{2,1,0:T(8,128)S(1)}, u32[]{:S(2)}, u32[]{:S(2)}) %collective-permute-start.1) | collective-permute-done | bytes 524320 | tf_op jit(solution)/shard_map/ppermute | solution.py:37
  62.3 13.4 %collective-permute-done.2 = f32[64,16,128]{2,1,0:T(8,128)S(1)} collective-permute-done((f32[64,16,128]{2,1,0:T(8,128)S(1)}, f32[64,16,128]{2,1,0:T(8,128)S(1)}, u32[]{:S(2)}, u32[]{:S(2)}) %collective-permute-start.2) | collective-permute-done | bytes 524320 | tf_op jit(solution)/shard_map/ppermute | solution.py:37
  75.7 3.0 %fusion.14 = f32[64,16,128]{2,1,0:T(8,128)} fusion(s32[]{:T(128)S(6)} %select_n.34, f32[64,16,128]{2,1,0:T(8,128)S(1)} %collective-permute-done.2, f32[64,16,128]{2,1,0:T(8,128)S(1)} %collective-permute-done.1, f32[64,16,128]{2,1,0:T(8,128)S(1)} %collective-permute-done, f32[64,16,128]{2,1,0:T(8,128)S(1)} %bitcast.112, bf16[512,512]{1,0:T(8,128)(2,1)S(1)} %copy-done, ...), kind=kOutput, calls=%fused_computation.30 | convolution fusion | flops 808976384 | bytes 2752520 | tf_op jit(solution)/shard_map/mak,ck->mac/dot_general | solution.py:42
  80.7 3.2 %all-to-all-start = ((f32[2,1,192]{2,1,0:T(1,128)}), f32[2,1,192]{2,1,0:T(1,128)S(1)}, u32[]{:S(2)}, u32[]{:S(2)}) async-start(f32[2,1,192]{2,1,0:T(1,128)} %reshape.675), calls=%async_computation | async-start | bytes 4096 | tf_op jit(solution)/shard_map/all_to_all | solution.py:103
  85.5 2.2 all-to-all-done
  88.5 10.0 %all-gather.3.cloned.1.call-done = f32[16,8,16,128]{3,2,1,0:T(8,128)} async-done(((f32[8,8,16,128]{3,2,1,0:T(8,128)}), f32[16,8,16,128]{3,2,1,0:T(8,128)}) %all-gather.3.cloned.1.call-update) | async-done | bytes 1048592 | tf_op jit(solution)/shard_map/all_gather | solution.py:84
  100.0 1.7 collective-permute-start.4
  104.7 2.4 collective-permute-start.6
  107.2 2.9 %collective-permute-done.5 = f32[8,18,1]{2,1,0:T(8,128)S(1)} collective-permute-done((f32[8,18,1]{2,1,0:T(8,128)S(1)}, f32[8,18,1]{2,1,0:T(8,128)S(1)}, u32[]{:S(2)}, u32[]{:S(2)}) %collective-permute-start.5) | collective-permute-done | bytes 608 | tf_op jit(solution)/shard_map/ppermute | solution.py:17
  110.1 2.0 collective-permute-done.6
  125.3 2.7 %collective-permute-start.10 = (f32[8,8,18,1]{2,1,3,0:T(8,128)S(1)}, f32[8,8,18,1]{2,1,3,0:T(8,128)S(1)}, u32[]{:S(2)}, u32[]{:S(2)}) collective-permute-start(f32[8,8,18,1]{2,1,3,0:T(8,128)S(1)} %copy.56), channel_id=1, source_target_pairs={{1,0},{2,1},{3,2},{0,3},{5,4},{6,5},{7,6},{4,7},{9,8},{10,9},{11,1... | collective-permute-start | bytes 13832 | tf_op jit(solution)/shard_map/ppermute | solution.py:18
  133.2 2.1 add_select_fusion
  138.1 20.4 %reduce-scatter.2.cloned.1.call-done = f32[8,8,16,128]{3,2,1,0:T(8,128)} async-done(((f32[16,8,16,128]{3,2,1,0:T(8,128)}), f32[8,8,16,128]{3,2,1,0:T(8,128)}) %reduce-scatter.2.cloned.1.call-update) | async-done | bytes 524304 | tf_op jit(solution)/shard_map/reduce_scatter | solution.py:128
  158.6 12.3 %all_to_all.83 = f32[64,16,128]{2,1,0:T(8,128)S(1)} all-to-all(f32[64,16,128]{2,1,0:T(8,128)} %bitcast.117), channel_id=1, replica_groups=mesh['tm'=2,'lat'=4,'lon'=4] {'lat'}, dimensions={0} | all-to-all | bytes 1048576 | tf_op jit(solution)/shard_map/all_to_all | solution.py:30
  171.6 11.2 %all_to_all.84 = f32[16,64,128]{2,0,1:T(8,128)S(1)} all-to-all(f32[16,64,128]{2,0,1:T(8,128)S(1)} %copy.62), channel_id=1, replica_groups=mesh['tm'=2,'lat'=4,'lon'=4] {'lat'}, dimensions={1} | all-to-all | bytes 1048576 | tf_op jit(solution)/shard_map/all_to_all | solution.py:33
  184.5 13.6 %collective-permute-done.11 = f32[64,16,128]{2,1,0:T(8,128)S(1)} collective-permute-done((f32[64,16,128]{2,1,0:T(8,128)S(1)}, f32[64,16,128]{2,1,0:T(8,128)S(1)}, u32[]{:S(2)}, u32[]{:S(2)}) %collective-permute-start.11) | collective-permute-done | bytes 524320 | tf_op jit(solution)/shard_map/ppermute | solution.py:37
  198.1 14.2 %collective-permute-done.12 = f32[64,16,128]{2,1,0:T(8,128)S(1)} collective-permute-done((f32[64,16,128]{2,1,0:T(8,128)S(1)}, f32[64,16,128]{2,1,0:T(8,128)S(1)}, u32[]{:S(2)}, u32[]{:S(2)}) %collective-permute-start.12) | collective-permute-done | bytes 524320 | tf_op jit(solution)/shard_map/ppermute | solution.py:37
  212.4 13.4 %collective-permute-done.13 = f32[64,16,128]{2,1,0:T(8,128)S(1)} collective-permute-done((f32[64,16,128]{2,1,0:T(8,128)S(1)}, f32[64,16,128]{2,1,0:T(8,128)S(1)}, u32[]{:S(2)}, u32[]{:S(2)}) %collective-permute-start.13) | collective-permute-done | bytes 524320 | tf_op jit(solution)/shard_map/ppermute | solution.py:37
  225.8 3.0 %fusion.4 = f32[64,16,128]{2,1,0:T(8,128)} fusion(s32[]{:T(128)S(6)} %select_n.34, f32[64,16,128]{2,1,0:T(8,128)S(1)} %collective-permute-done.13, f32[64,16,128]{2,1,0:T(8,128)S(1)} %collective-permute-done.12, f32[64,16,128]{2,1,0:T(8,128)S(1)} %collective-permute-done.11, f32[64,16,128]{2,1,0:T(8,128)S(1)} %bitcast.115, ...), kind=kOutput, calls=%fused_computation.22 | convolution fusion | flops 808976384 | bytes 2752520 | tf_op jit(solution)/shard_map/mak,ck->mac/dot_general | solution.py:42
  228.8 18.9 %all-gather.5.cloned.1.call-done = f32[16,8,16,128]{3,2,1,0:T(8,128)} async-done(((f32[8,8,16,128]{3,2,1,0:T(8,128)}), f32[16,8,16,128]{3,2,1,0:T(8,128)}) %all-gather.5.cloned.1.call-update) | async-done | bytes 1048592 | tf_op jit(solution)/shard_map/all_gather | solution.py:132
  247.7 2.3 add.135
  (131 shorter events, 36.0 us)
Async XLA Ops:
  6.5 69.2 %copy-start = (bf16[512,512]{1,0:T(8,128)(2,1)S(1)}, bf16[512,512]{1,0:T(8,128)(2,1)}, u32[]{:S(2)}) copy-start(bf16[512,512]{1,0:T(8,128)(2,1)} %param.47) | copy-start | bytes 1572868
  6.5 92.0 %all-gather.3.cloned.1.call-start = ((), (), s32[]{:S(2)}) async-start(), calls=%async_computation.6 | async-start | bytes 1572864 | tf_op jit(solution)/shard_map/all_gather | solution.py:84
  21.4 40.9 %copy-start.6 = (s32[1,2,1,1,64]{4,3,2,1,0:T(1,128)S(1)}, s32[1,2,1,1,64]{4,3,2,1,0:T(1,128)}, u32[]{:S(2)}) copy-start(s32[1,2,1,1,64]{4,3,2,1,0:T(1,128)} %param.50) | copy-start | bytes 1540
  32.8 15.2 %collective-permute-start = (f32[64,16,128]{2,1,0:T(8,128)S(1)}, f32[64,16,128]{2,1,0:T(8,128)S(1)}, u32[]{:S(2)}, u32[]{:S(2)}) collective-permute-start(f32[64,16,128]{2,1,0:T(8,128)S(1)} %bitcast.111), channel_id=1, source_target_pairs={{0,1},{1,2},{2,3},{3,0},{4,5},{5,6},{6,7},{7,4},{8,9},{9,10},{10,1... | collective-permute-start | bytes 1572872 | tf_op jit(solution)/shard_map/ppermute | solution.py:37
  48.0 14.3 %collective-permute-start.1 = (f32[64,16,128]{2,1,0:T(8,128)S(1)}, f32[64,16,128]{2,1,0:T(8,128)S(1)}, u32[]{:S(2)}, u32[]{:S(2)}) collective-permute-start(f32[64,16,128]{2,1,0:T(8,128)S(1)} %collective-permute-done), channel_id=1, source_target_pairs={{0,1},{1,2},{2,3},{3,0},{4,5},{5,6},{6,7},{7,4},{8,9},{9,10},{10,1... | collective-permute-start | bytes 1572872 | tf_op jit(solution)/shard_map/ppermute | solution.py:37
  62.3 13.4 %collective-permute-start.2 = (f32[64,16,128]{2,1,0:T(8,128)S(1)}, f32[64,16,128]{2,1,0:T(8,128)S(1)}, u32[]{:S(2)}, u32[]{:S(2)}) collective-permute-start(f32[64,16,128]{2,1,0:T(8,128)S(1)} %collective-permute-done.1), channel_id=1, source_target_pairs={{0,1},{1,2},{2,3},{3,0},{4,5},{5,6},{6,7},{7,4},{8,9},{9,10},{10,1... | collective-permute-start | bytes 1572872 | tf_op jit(solution)/shard_map/ppermute | solution.py:37
  62.3 22.4 %copy-start.10 = (s32[3]{0:T(128)S(1)}, s32[3]{0:T(128)}, u32[]{:S(2)}) copy-start(s32[3]{0:T(128)} %constant.449.clone.1) | copy-start | bytes 40
  62.3 36.2 %copy-start.2 = (bf16[1,16,8,16,128]{4,3,2,1,0:T(8,128)(2,1)S(1)}, bf16[1,16,8,16,128]{4,3,2,1,0:T(8,128)(2,1)}, u32[]{:S(2)}) copy-start(bf16[1,16,8,16,128]{4,3,2,1,0:T(8,128)(2,1)} %param.45) | copy-start | bytes 1572868
  78.7 33.4 %copy-start.5 = (f32[32,18]{0,1:T(8,128)S(1)}, f32[32,18]{0,1:T(8,128)}, u32[]{:S(2)}) copy-start(f32[32,18]{0,1:T(8,128)} %param.48) | copy-start | bytes 6916
  80.7 7.0 %all-to-all-start = ((f32[2,1,192]{2,1,0:T(1,128)}), f32[2,1,192]{2,1,0:T(1,128)S(1)}, u32[]{:S(2)}, u32[]{:S(2)}) async-start(f32[2,1,192]{2,1,0:T(1,128)} %reshape.675), calls=%async_computation | async-start | bytes 4096 | tf_op jit(solution)/shard_map/all_to_all | solution.py:103
  83.9 74.6 %reduce-scatter.2.cloned.1.call-start = ((), (), s32[]{:S(2)}) async-start(), calls=%async_computation.7 | async-start | bytes 1572864 | tf_op jit(solution)/shard_map/reduce_scatter | solution.py:128
  88.5 24.2 %copy-start.3 = (f32[256,130]{0,1:T(8,128)S(1)}, f32[256,130]{0,1:T(8,128)}, u32[]{:S(2)}) copy-start(f32[256,130]{0,1:T(8,128)} %param.49) | copy-start | bytes 399364
  99.9 3.1 %collective-permute-start.3 = (f32[8,1,128]{2,1,0:T(1,128)S(1)}, f32[8,1,128]{2,1,0:T(1,128)S(1)}, u32[]{:S(2)}, u32[]{:S(2)}) collective-permute-start(f32[8,1,128]{2,1,0:T(1,128)S(1)} %get-tuple-element.223), channel_id=1, source_target_pairs={{0,4},{4,8},{8,12},{12,0},{1,5},{5,9},{9,13},{13,1},{2,6},{6,10},{... | collective-permute-start | bytes 12296 | tf_op jit(solution)/shard_map/ppermute | solution.py:17
  100.0 3.1 %collective-permute-start.4 = (f32[8,1,128]{2,1,0:T(1,128)S(1)}, f32[8,1,128]{2,1,0:T(1,128)S(1)}, u32[]{:S(2)}, u32[]{:S(2)}) collective-permute-start(f32[8,1,128]{2,1,0:T(1,128)S(1)} %get-tuple-element.224), channel_id=1, source_target_pairs={{4,0},{8,4},{12,8},{0,12},{5,1},{9,5},{13,9},{1,13},{6,2},{10,6},{... | collective-permute-start | bytes 12296 | tf_op jit(solution)/shard_map/ppermute | solution.py:18
  103.2 7.0 %collective-permute-start.5 = (f32[8,18,1]{2,1,0:T(8,128)S(1)}, f32[8,18,1]{2,1,0:T(8,128)S(1)}, u32[]{:S(2)}, u32[]{:S(2)}) collective-permute-start(f32[8,18,1]{2,1,0:T(8,128)S(1)} %get-tuple-element.221), channel_id=1, source_target_pairs={{0,1},{1,2},{2,3},{3,0},{4,5},{5,6},{6,7},{7,4},{8,9},{9,10},{10,1... | collective-permute-start | bytes 1736 | tf_op jit(solution)/shard_map/ppermute | solution.py:17
  104.7 7.5 %collective-permute-start.6 = (f32[8,18,1]{2,1,0:T(8,128)S(1)}, f32[8,18,1]{2,1,0:T(8,128)S(1)}, u32[]{:S(2)}, u32[]{:S(2)}) collective-permute-start(f32[8,18,1]{2,1,0:T(8,128)S(1)} %get-tuple-element.222), channel_id=1, source_target_pairs={{1,0},{2,1},{3,2},{0,3},{5,4},{6,5},{7,6},{4,7},{9,8},{10,9},{11,1... | collective-permute-start | bytes 1736 | tf_op jit(solution)/shard_map/ppermute | solution.py:18
  119.5 3.3 %collective-permute-start.7 = (f32[8,8,1,128]{3,1,2,0:T(8,128)S(1)}, f32[8,8,1,128]{3,1,2,0:T(8,128)S(1)}, u32[]{:S(2)}, u32[]{:S(2)}) collective-permute-start(f32[8,8,1,128]{3,1,2,0:T(8,128)S(1)} %get-tuple-element.212), channel_id=1, source_target_pairs={{0,4},{4,8},{8,12},{12,0},{1,5},{5,9},{9,13},{13,1},{2,6},{6,10},{... | collective-permute-start | bytes 98312 | tf_op jit(solution)/shard_map/ppermute | solution.py:17
  119.7 3.2 %collective-permute-start.8 = (f32[8,8,1,128]{3,1,2,0:T(8,128)S(1)}, f32[8,8,1,128]{3,1,2,0:T(8,128)S(1)}, u32[]{:S(2)}, u32[]{:S(2)}) collective-permute-start(f32[8,8,1,128]{3,1,2,0:T(8,128)S(1)} %get-tuple-element.213), channel_id=1, source_target_pairs={{4,0},{8,4},{12,8},{0,12},{5,1},{9,5},{13,9},{1,13},{6,2},{10,6},{... | collective-permute-start | bytes 98312 | tf_op jit(solution)/shard_map/ppermute | solution.py:18
  123.6 5.9 %collective-permute-start.9 = (f32[8,8,18,1]{2,1,3,0:T(8,128)S(1)}, f32[8,8,18,1]{2,1,3,0:T(8,128)S(1)}, u32[]{:S(2)}, u32[]{:S(2)}) collective-permute-start(f32[8,8,18,1]{2,1,3,0:T(8,128)S(1)} %copy.55), channel_id=1, source_target_pairs={{0,1},{1,2},{2,3},{3,0},{4,5},{5,6},{6,7},{7,4},{8,9},{9,10},{10,1... | collective-permute-start | bytes 13832 | tf_op jit(solution)/shard_map/ppermute | solution.py:17
  125.3 5.0 %collective-permute-start.10 = (f32[8,8,18,1]{2,1,3,0:T(8,128)S(1)}, f32[8,8,18,1]{2,1,3,0:T(8,128)S(1)}, u32[]{:S(2)}, u32[]{:S(2)}) collective-permute-start(f32[8,8,18,1]{2,1,3,0:T(8,128)S(1)} %copy.56), channel_id=1, source_target_pairs={{1,0},{2,1},{3,2},{0,3},{5,4},{6,5},{7,6},{4,7},{9,8},{10,9},{11,1... | collective-permute-start | bytes 13832 | tf_op jit(solution)/shard_map/ppermute | solution.py:18
  138.1 109.6 %all-gather.5.cloned.1.call-start = ((), (), s32[]{:S(2)}) async-start(), calls=%async_computation.8 | async-start | bytes 1572864 | tf_op jit(solution)/shard_map/all_gather | solution.py:132
  183.0 15.1 %collective-permute-start.11 = (f32[64,16,128]{2,1,0:T(8,128)S(1)}, f32[64,16,128]{2,1,0:T(8,128)S(1)}, u32[]{:S(2)}, u32[]{:S(2)}) collective-permute-start(f32[64,16,128]{2,1,0:T(8,128)S(1)} %bitcast.114), channel_id=1, source_target_pairs={{0,1},{1,2},{2,3},{3,0},{4,5},{5,6},{6,7},{7,4},{8,9},{9,10},{10,1... | collective-permute-start | bytes 1572872 | tf_op jit(solution)/shard_map/ppermute | solution.py:37
  198.1 14.2 %collective-permute-start.12 = (f32[64,16,128]{2,1,0:T(8,128)S(1)}, f32[64,16,128]{2,1,0:T(8,128)S(1)}, u32[]{:S(2)}, u32[]{:S(2)}) collective-permute-start(f32[64,16,128]{2,1,0:T(8,128)S(1)} %collective-permute-done.11), channel_id=1, source_target_pairs={{0,1},{1,2},{2,3},{3,0},{4,5},{5,6},{6,7},{7,4},{8,9},{9,10},{10,1... | collective-permute-start | bytes 1572872 | tf_op jit(solution)/shard_map/ppermute | solution.py:37
  212.4 13.4 %collective-permute-start.13 = (f32[64,16,128]{2,1,0:T(8,128)S(1)}, f32[64,16,128]{2,1,0:T(8,128)S(1)}, u32[]{:S(2)}, u32[]{:S(2)}) collective-permute-start(f32[64,16,128]{2,1,0:T(8,128)S(1)} %collective-permute-done.12), channel_id=1, source_target_pairs={{0,1},{1,2},{2,3},{3,0},{4,5},{5,6},{6,7},{7,4},{8,9},{9,10},{10,1... | collective-permute-start | bytes 1572872 | tf_op jit(solution)/shard_map/ppermute | solution.py:37
  (5 other events, 84.3 us)
Sparse Core Ops, SparseCore 0:
  78.9 19.6 all-gather.2
  138.2 20.3 reduce-scatter.1
  228.9 18.7 all-gather.4
